TPU v7x, 32 devices: a whole 2x2x4 slice. The times are simulated.
32 devices in a mesh: seq: 2 (over x), batch: 4 (over y, core), head: 4 (over z).
Axes of the slice: x: 2, y: 2, z: 4, core: 2. Of those that a mesh axis runs over, the one named last changes fastest.
Arguments:
- hidden: bfloat16 [4, 256, 16384], P('batch', None, 'seq'), may hold values from -760 to 760
- gain: float32 [16384], P('seq'), may hold values from 0.5 to 1.5
- key_weight: bfloat16 [16384, 1024], P('seq', 'head'), may hold values from -0.046875 to 0.046875
- value_weight: bfloat16 [16384, 1024], P('seq', 'head'), may hold values from -0.046875 to 0.046875
- positions: int32 [4, 256], P('batch', 'seq'), may hold values from 0 to 32767
- initial_basis: float32 [2048, 256], P('head'), may hold values from -6 to 6
Outputs:
- basis: float32 [2048, 256], P('head')
All inputs are finite; a program needn't handle non-finite values.
Results may differ from a plain program's by a relative error of at most 0.0063.
Values may be sent and summed in bfloat16 or wider, within the bound.
A program may use at most 64 MiB of HBM per device.

v0:
```python
import math
import jax
import jax.numpy as jnp
from jax import lax
from jax.sharding import PartitionSpec as P

D = 16384
HEAD_DIM = 128
ITERS = 4
EPSILON = 1e-05
ROTARY_BASE = 500000.0


def rotary(head_rows, position_row):
    half_width = head_rows.shape[-1] // 2
    index_row = jnp.arange(half_width, dtype=jnp.float32)
    frequency = jnp.exp(index_row * (-math.log(ROTARY_BASE) / half_width))
    angles = position_row.astype(jnp.float32)[:, None] * frequency[None, :]
    cosine = jnp.cos(angles)[:, None, :]
    sine_part = jnp.sin(angles)[:, None, :]
    first_half = head_rows[..., :half_width]
    second_half = head_rows[..., half_width:]
    return jnp.concatenate(
        [
            first_half * cosine - second_half * sine_part,
            second_half * cosine + first_half * sine_part,
        ],
        axis=-1,
    )


def whole_of(basis_block):
    return lax.all_gather(basis_block, "head", axis=0, tiled=True)


def total_squares(local_squares, local_tokens):
    all_squares = lax.psum(local_squares, "seq")
    return lax.dynamic_slice_in_dim(all_squares, lax.axis_index("seq") * local_tokens, local_tokens)


def gram_of(images):
    return lax.dot_general(
        images,
        images,
        (((0,), (0,)), ((), ())),
        precision=lax.Precision.HIGHEST,
        preferred_element_type=jnp.float32,
    )


def orthonormal(images, gram_matrix):
    factor = jnp.linalg.cholesky(gram_matrix)
    return lax.linalg.triangular_solve(
        factor, images, left_side=False, lower=True, transpose_a=True
    )


def body(hidden, gain, key_weight, value_weight, positions, initial_basis):
    hidden_rows = hidden[0]
    local_tokens = positions.shape[1]
    widened = hidden_rows.astype(jnp.float32)
    scaled = (widened * gain).astype(jnp.bfloat16)
    local_squares = jnp.sum(widened * widened, axis=1)
    key_columns = key_weight.shape[1]
    weights = jnp.concatenate([key_weight, value_weight], axis=1)
    own_squares = total_squares(local_squares, local_tokens)
    projected = lax.psum_scatter(
        jnp.dot(scaled, weights, preferred_element_type=jnp.float32),
        "seq",
        scatter_dimension=0,
        tiled=True,
    )
    inverse_scale = lax.rsqrt(own_squares / D + EPSILON)
    projected = projected * inverse_scale[:, None]
    key_rows = rotary(projected[:, :key_columns].reshape(local_tokens, -1, HEAD_DIM), positions[0])
    value_rows = projected[:, key_columns:].reshape(local_tokens, -1, HEAD_DIM)
    joint_rows = (
        jnp.stack([key_rows, value_rows], axis=2).reshape(local_tokens, -1).astype(jnp.bfloat16)
    )
    partial_value = lax.dot_general(
        joint_rows,
        lax.all_gather(joint_rows, "head", axis=1, tiled=True),
        (((0,), (0,)), ((), ())),
        preferred_element_type=jnp.float32,
    )
    token_total = local_tokens * lax.axis_size("seq") * lax.axis_size("batch")
    basis_block = initial_basis
    covariance = lax.psum(partial_value, ("seq", "batch")) / token_total
    for iteration in range(ITERS):
        whole_basis = whole_of(basis_block)
        images = jnp.dot(
            covariance,
            whole_basis,
            precision=lax.Precision.HIGHEST,
            preferred_element_type=jnp.float32,
        )
        gram_matrix = lax.psum(gram_of(images), "head") / whole_basis.shape[0]
        basis_block = orthonormal(images, gram_matrix)
    return basis_block


def solution(mesh):
    return jax.shard_map(
        body,
        mesh=mesh,
        in_specs=(
            P("batch", None, "seq"),
            P("seq"),
            P("seq", "head"),
            P("seq", "head"),
            P("batch", "seq"),
            P("head", None),
        ),
        out_specs=P("head", None),
        check_vma=False,
    )
```

profile of v0, /device:TPU:0, one launch (start us, length us, event | category | flops | bytes accessed | tf_op | source)
XLA Modules:
  0.0 718.3 jit_solution(16877559719014018275)
XLA Ops:
  7.4 7.8 %fusion.2 = f32[256,512]{1,0:T(8,128)} fusion(bf16[8192,256]{1,0:T(8,128)(2,1)} %param.12, bf16[8192,256]{1,0:T(8,128)(2,1)} %param.11, bf16[1,256,8192]{2,1,0:T(8,128)(2,1)} %param.9, f32[8192]{0:T(1024)} %param.10), kind=kOutput, calls=%fused_computation.12 | convolution fusion | flops 2170552320 | bytes 13139968 | tf_op jit(solution)/shard_map/dot_general | solution.py:68
  15.2 3.1 fusion.1
  18.4 5.9 psum.42
  24.5 8.2 %reduce-scatter.2.cloned.1.call-done = f32[128,512]{1,0:T(8,128)} async-done(((f32[256,512]{1,0:T(8,128)}), f32[128,512]{1,0:T(8,128)}) %reduce-scatter.2.cloned.1.call-update) | async-done | bytes 262160 | tf_op jit(solution)/shard_map/reduce_scatter | solution.py:67
  32.7 1.0 broadcast_multiply_fusion.4
  34.1 15.5 %all_gather.15 = bf16[128,2048]{0,1:T(8,128)(2,1)S(1)} all-gather(bf16[128,512]{0,1:T(8,128)(2,1)S(1)} %bitcast.160), channel_id=1, replica_groups=mesh['seq'=2,'batch'=4,'head'=4] {'head'}, dimensions={1}, use_global_device_ids=true | all-gather | bytes 655360 | tf_op jit(solution)/shard_map/all_gather | solution.py:82
  49.6 2.7 fusion.74
  52.9 81.2 %all-reduce.7.cloned.1.call-done = f32[512,2048]{1,0:T(8,128)} async-done(((f32[512,2048]{1,0:T(8,128)}), f32[512,2048]{1,0:T(8,128)}) %all-reduce.7.cloned.1.call-update) | async-done | bytes 4194320 | tf_op jit(solution)/shard_map/psum | solution.py:88
  134.1 6.1 fusion.15
  140.2 1.7 fusion.75
  142.3 35.4 %all-reduce.9.cloned.1.call-done = f32[256,256]{0,1:T(8,128)} async-done(((f32[256,256]{0,1:T(8,128)}), f32[256,256]{0,1:T(8,128)}) %all-reduce.9.cloned.1.call-update) | async-done | bytes 262160 | tf_op jit(solution)/shard_map/psum | solution.py:97
  177.7 1.0 broadcast_multiply_fusion.3
  178.8 1.0 fusion.32
  179.8 11.7 %cholesky.214 = f32[128,128]{1,0:T(8,128)S(1)} custom-call(f32[128,128]{1,0:T(8,128)S(1)} %cholesky.346), custom_call_target="Cholesky" | custom-call | tf_op jit(solution)/shard_map/jit(cholesky)/cholesky | solution.py:52
  191.5 9.8 %custom-call.17 = f32[1,128,128]{1,2,0:T(8,128)S(1)} custom-call(f32[1,128,128]{2,1,0:T(8,128)S(1)} %get-tuple-element.94), custom_call_target="InvertDiagBlocksLowerTriangular" | custom-call | tf_op jit(solution)/shard_map/jit(cholesky)/cholesky | solution.py:52
  201.8 11.7 %cholesky.231 = f32[128,128]{1,0:T(8,128)S(1)} custom-call(f32[128,128]{1,0:T(8,128)S(1)} %convolution_subtract_fusion.7), custom_call_target="Cholesky" | custom-call | tf_op jit(solution)/shard_map/jit(cholesky)/cholesky | solution.py:52
  215.6 4.5 while.8
  216.8 1.4 bitcast_dynamic-update-slice_fusion.8
  218.7 1.4 bitcast_dynamic-update-slice_fusion.8
  220.1 19.7 %custom-call.18 = f32[2,128,128]{1,2,0:T(8,128)S(1)} custom-call(f32[2,128,128]{2,1,0:T(8,128)S(1)} %get-tuple-element.33), custom_call_target="InvertDiagBlocksLowerTriangular" | custom-call | tf_op jit(solution)/shard_map/triangular_solve/custom-call.0 | solution.py:53
  241.2 0.8 pad_maximum_fusion
  242.1 45.1 %all-gather.7.cloned.1.call-done = f32[2048,256]{0,1:T(8,128)} async-done(((f32[512,256]{0,1:T(8,128)}), f32[2048,256]{0,1:T(8,128)}) %all-gather.7.cloned.1.call-update) | async-done | bytes 2097168 | tf_op jit(solution)/shard_map/all_gather | solution.py:33
  287.2 6.1 fusion.13
  293.3 1.7 fusion.76
  295.3 34.3 %all-reduce.11.cloned.1.call-done = f32[256,256]{0,1:T(8,128)} async-done(((f32[256,256]{0,1:T(8,128)}), f32[256,256]{0,1:T(8,128)}) %all-reduce.11.cloned.1.call-update) | async-done | bytes 262160 | tf_op jit(solution)/shard_map/psum | solution.py:97
  329.5 1.0 broadcast_multiply_fusion.2
  330.6 1.0 fusion.31
  331.6 11.7 %cholesky.248 = f32[128,128]{1,0:T(8,128)S(1)} custom-call(f32[128,128]{1,0:T(8,128)S(1)} %cholesky.349), custom_call_target="Cholesky" | custom-call | tf_op jit(solution)/shard_map/jit(cholesky)/cholesky | solution.py:52
  343.4 9.8 %custom-call.19 = f32[1,128,128]{1,2,0:T(8,128)S(1)} custom-call(f32[1,128,128]{2,1,0:T(8,128)S(1)} %get-tuple-element.90), custom_call_target="InvertDiagBlocksLowerTriangular" | custom-call | tf_op jit(solution)/shard_map/jit(cholesky)/cholesky | solution.py:52
  353.7 11.7 %cholesky.265 = f32[128,128]{1,0:T(8,128)S(1)} custom-call(f32[128,128]{1,0:T(8,128)S(1)} %convolution_subtract_fusion.6), custom_call_target="Cholesky" | custom-call | tf_op jit(solution)/shard_map/jit(cholesky)/cholesky | solution.py:52
  368.1 4.2 while.9
  368.9 1.4 bitcast_dynamic-update-slice_fusion.9
  370.9 1.4 bitcast_dynamic-update-slice_fusion.9
  372.2 19.7 %custom-call.20 = f32[2,128,128]{1,2,0:T(8,128)S(1)} custom-call(f32[2,128,128]{2,1,0:T(8,128)S(1)} %get-tuple-element.34), custom_call_target="InvertDiagBlocksLowerTriangular" | custom-call | tf_op jit(solution)/shard_map/triangular_solve/custom-call.0 | solution.py:53
  393.4 0.8 pad_maximum_fusion.1
  394.3 45.1 %all-gather.9.cloned.1.call-done = f32[2048,256]{0,1:T(8,128)} async-done(((f32[512,256]{0,1:T(8,128)}), f32[2048,256]{0,1:T(8,128)}) %all-gather.9.cloned.1.call-update) | async-done | bytes 2097168 | tf_op jit(solution)/shard_map/all_gather | solution.py:33
  439.4 6.1 fusion.11
  445.4 1.7 fusion.77
  447.5 34.1 %all-reduce.13.cloned.1.call-done = f32[256,256]{0,1:T(8,128)} async-done(((f32[256,256]{0,1:T(8,128)}), f32[256,256]{0,1:T(8,128)}) %all-reduce.13.cloned.1.call-update) | async-done | bytes 262160 | tf_op jit(solution)/shard_map/psum | solution.py:97
  481.6 1.0 broadcast_multiply_fusion.1
  482.7 1.0 fusion.30
  483.7 11.7 %cholesky.282 = f32[128,128]{1,0:T(8,128)S(1)} custom-call(f32[128,128]{1,0:T(8,128)S(1)} %cholesky.352), custom_call_target="Cholesky" | custom-call | tf_op jit(solution)/shard_map/jit(cholesky)/cholesky | solution.py:52
  495.5 9.8 %custom-call.21 = f32[1,128,128]{1,2,0:T(8,128)S(1)} custom-call(f32[1,128,128]{2,1,0:T(8,128)S(1)} %get-tuple-element.86), custom_call_target="InvertDiagBlocksLowerTriangular" | custom-call | tf_op jit(solution)/shard_map/jit(cholesky)/cholesky | solution.py:52
  505.8 11.7 %cholesky.299 = f32[128,128]{1,0:T(8,128)S(1)} custom-call(f32[128,128]{1,0:T(8,128)S(1)} %convolution_subtract_fusion.5), custom_call_target="Cholesky" | custom-call | tf_op jit(solution)/shard_map/jit(cholesky)/cholesky | solution.py:52
  520.2 15.9 %while.10 = (s32[]{:T(128)}, f32[256,256]{1,0:T(8,128)S(1)}, s32[2,2]{1,0:T(2,128)S(1)}, f32[2,128,128]{2,1,0:T(8,128)S(1)}, s32[]{:T(128)}) while((s32[]{:T(128)}, f32[256,256]{1,0:T(8,128)S(1)}, s32[2,2]{1,0:T(2,128)S(1)}, f32[2,128,128]{2,1,0:T(8,128)S(1)}, s32[]{:T(128)}) %tuple.112), condition=%wide.while_cond.clone.1, body=%wide.while_body.clone.1.sunk | while | flops 2 | bytes 131181 | solution.py:53
  532.7 1.4 bitcast_dynamic-update-slice_fusion.10
  534.7 1.4 bitcast_dynamic-update-slice_fusion.10
  536.1 19.7 %custom-call.22 = f32[2,128,128]{1,2,0:T(8,128)S(1)} custom-call(f32[2,128,128]{2,1,0:T(8,128)S(1)} %get-tuple-element.35), custom_call_target="InvertDiagBlocksLowerTriangular" | custom-call | tf_op jit(solution)/shard_map/triangular_solve/custom-call.0 | solution.py:53
  557.2 0.8 pad_maximum_fusion.2
  558.1 45.1 %all-gather.11.cloned.1.call-done = f32[2048,256]{0,1:T(8,128)} async-done(((f32[512,256]{0,1:T(8,128)}), f32[2048,256]{0,1:T(8,128)}) %all-gather.11.cloned.1.call-update) | async-done | bytes 2097168 | tf_op jit(solution)/shard_map/all_gather | solution.py:33
  603.2 6.1 fusion.9
  609.3 1.7 fusion.78
  611.0 34.5 %all-reduce.15.cloned.1.call-done = f32[256,256]{0,1:T(8,128)} async-done(((f32[256,256]{0,1:T(8,128)}), f32[256,256]{0,1:T(8,128)}) %all-reduce.15.cloned.1.call-update) | async-done | bytes 262160 | tf_op jit(solution)/shard_map/psum | solution.py:97
  645.5 1.0 broadcast_multiply_fusion
  646.6 1.0 fusion.29
  647.6 11.7 %cholesky.316 = f32[128,128]{1,0:T(8,128)S(1)} custom-call(f32[128,128]{1,0:T(8,128)S(1)} %cholesky.355), custom_call_target="Cholesky" | custom-call | tf_op jit(solution)/shard_map/jit(cholesky)/cholesky | solution.py:52
  659.4 9.8 %custom-call.23 = f32[1,128,128]{1,2,0:T(8,128)S(1)} custom-call(f32[1,128,128]{2,1,0:T(8,128)S(1)} %get-tuple-element.82), custom_call_target="InvertDiagBlocksLowerTriangular" | custom-call | tf_op jit(solution)/shard_map/jit(cholesky)/cholesky | solution.py:52
  669.7 11.7 %cholesky.333 = f32[128,128]{1,0:T(8,128)S(1)} custom-call(f32[128,128]{1,0:T(8,128)S(1)} %convolution_subtract_fusion.4), custom_call_target="Cholesky" | custom-call | tf_op jit(solution)/shard_map/jit(cholesky)/cholesky | solution.py:52
  681.4 0.7 compare_reduce_fusion
  684.2 4.1 while.11
  684.8 1.4 bitcast_dynamic-update-slice_fusion.11
  686.8 1.4 bitcast_dynamic-update-slice_fusion.11
  688.3 19.9 %custom-call.24 = f32[2,128,128]{1,2,0:T(8,128)S(1)} custom-call(f32[2,128,128]{2,1,0:T(8,128)S(1)} %get-tuple-element.36), custom_call_target="InvertDiagBlocksLowerTriangular" | custom-call | tf_op jit(solution)/shard_map/triangular_solve/custom-call.0 | solution.py:53
  709.7 1.0 copy.27
  (107 shorter events, 19.8 us)
Async XLA Ops:
  7.4 25.3 %reduce-scatter.2.cloned.1.call-start = ((), (), s32[]{:S(2)}) async-start(), calls=%async_computation.1 | async-start | bytes 786432 | tf_op jit(solution)/shard_map/reduce_scatter | solution.py:67
  15.2 9.1 %copy-start = (s32[1,128]{1,0:T(1,128)S(1)}, s32[1,128]{1,0:T(1,128)}, u32[]{:S(2)}) copy-start(s32[1,128]{1,0:T(1,128)} %param.13) | copy-start | bytes 1540
  15.2 118.9 %all-reduce.7.cloned.1.call-start = ((), (), s32[]{:S(2)}) async-start(), calls=%async_computation.2 | async-start | bytes 8388608 | tf_op jit(solution)/shard_map/psum | solution.py:88
  52.3 81.8 %all-gather.5.cloned.1.call-start = ((), (), s32[]{:S(2)}) async-start(), calls=%async_computation.3 | async-start | bytes 2621440 | tf_op jit(solution)/shard_map/all_gather | solution.py:33
  52.9 124.8 %all-reduce.9.cloned.1.call-start = ((), (), s32[]{:S(2)}) async-start(), calls=%async_computation.4 | async-start | bytes 524288 | tf_op jit(solution)/shard_map/psum | solution.py:97
  141.9 145.3 %all-gather.7.cloned.1.call-start = ((), (), s32[]{:S(2)}) async-start(), calls=%async_computation.5 | async-start | bytes 2621440 | tf_op jit(solution)/shard_map/all_gather | solution.py:33
  242.1 87.4 %all-reduce.11.cloned.1.call-start = ((), (), s32[]{:S(2)}) async-start(), calls=%async_computation.6 | async-start | bytes 524288 | tf_op jit(solution)/shard_map/psum | solution.py:97
  295.0 144.3 %all-gather.9.cloned.1.call-start = ((), (), s32[]{:S(2)}) async-start(), calls=%async_computation.7 | async-start | bytes 2621440 | tf_op jit(solution)/shard_map/all_gather | solution.py:33
  394.2 87.4 %all-reduce.13.cloned.1.call-start = ((), (), s32[]{:S(2)}) async-start(), calls=%async_computation.8 | async-start | bytes 524288 | tf_op jit(solution)/shard_map/psum | solution.py:97
  447.2 156.0 %all-gather.11.cloned.1.call-start = ((), (), s32[]{:S(2)}) async-start(), calls=%async_computation.9 | async-start | bytes 2621440 | tf_op jit(solution)/shard_map/all_gather | solution.py:33
  558.0 87.4 %all-reduce.15.cloned.1.call-start = ((), (), s32[]{:S(2)}) async-start(), calls=%async_computation.10 | async-start | bytes 524288 | tf_op jit(solution)/shard_map/psum | solution.py:97
Sparse Core Ops, SparseCore 0:
  15.3 17.3 reduce-scatter.1
  52.4 81.6 all-reduce.6
Sparse Core Ops, SparseCore 1:
  54.3 46.3 all-gather.4
  142.0 35.6 all-reduce.8
  242.2 45.0 all-gather.6
  295.1 34.3 all-reduce.10
  394.3 45.0 all-gather.8
  447.3 34.3 all-reduce.12
  558.1 45.0 all-gather.10
  611.1 34.3 all-reduce.14
where the time goes:
time: 725 us; the launch traced here: 718 us
  waiting for transfers between devices  364 us (50%)
  other arithmetic  232 us (32%)
  matrix products  49.2 us (7%)
  blocking collectives  21.4 us (3%)
  between operations  20.9 us (3%)
  local copies, waits for them, and re-layouts  17.7 us (2%)
  loops' own time  12.9 us (2%)
    psum x4, waiting for transfers between devices, body(): gram_matrix = lax.psum(gram_of(images), 'head') / whole_basis.shape[0]  138 us
    another operation x27, other arithmetic, orthonormal(): factor = jnp.linalg.cholesky(gram_matrix)  138 us
    all_gather x4, waiting for transfers between devices, whole_of(): return lax.all_gather(basis_block, 'head', axis=0, tiled=True)  135 us
    another operation x13, other arithmetic, orthonormal(): lax.linalg.triangular_solve(factor, images, left_side=False, lower=True,...  81.6 us
    psum x1, waiting for transfers between devices, body(): covariance = lax.psum(partial_value, ('seq', 'batch')) / token_total  81.2 us
    dot_general x4, matrix products, body(): jnp.dot(covariance, whole_basis, precision=lax.Precision.HIGHEST, preferr...  24.3 us
    another operation x30, local copies, waits for them, and re-layouts, orthonormal(): lax.linalg.triangular_solve(factor, images, left_side=False, lower=True,...  16.8 us
    all_gather x1, blocking collectives, body(): lax.all_gather(joint_rows, 'head', axis=1, tiled=True)  15.5 us
  transfers between devices with their start and end apart: 10, of which 9 were waited for; matrix products, arithmetic and copies ran while one was open for 0% of the time, Pallas kernels for 0%

commit v1 on v0

--- a/solution.py
+++ b/solution.py
@@ -94,7 +94,9 @@
             precision=lax.Precision.HIGHEST,
             preferred_element_type=jnp.float32,
         )
-        gram_matrix = lax.psum(gram_of(images), "head") / whole_basis.shape[0]
+        gram_matrix = (
+            jnp.sum(lax.all_gather(gram_of(images), "head"), axis=0) / whole_basis.shape[0]
+        )
         basis_block = orthonormal(images, gram_matrix)
     return basis_block
 

time: 725 us -> 692 us (0.954)
  waiting for transfers between devices: 364 us -> 332 us
    psum x4 -> x0, waiting for transfers between devices: 138 us -> none  [body(): gram_matrix = lax.psum(gram_of(images), 'head') / whole_basis.shape[0]]
    all_gather x0 -> x4, waiting for transfers between devices: none -> 108 us  [body(): lax.all_gather(gram_of(images), 'head')]
where the time goes in v1:
time: 692 us; the launch traced here: 686 us
  waiting for transfers between devices  332 us (48%)
  other arithmetic  229 us (33%)
  matrix products  49.3 us (7%)
  blocking collectives  21.4 us (3%)
  between operations  20.9 us (3%)
  local copies, waits for them, and re-layouts  18.2 us (3%)
  loops' own time  13 us (2%)
    another operation x27, other arithmetic, orthonormal(): factor = jnp.linalg.cholesky(gram_matrix)  138 us
    all_gather x4, waiting for transfers between devices, whole_of(): return lax.all_gather(basis_block, 'head', axis=0, tiled=True)  135 us
    all_gather x4, waiting for transfers between devices, body(): lax.all_gather(gram_of(images), 'head')  108 us
    another operation x13, other arithmetic, orthonormal(): lax.linalg.triangular_solve(factor, images, left_side=False, lower=True,...  81.6 us
    psum x1, waiting for transfers between devices, body(): covariance = lax.psum(partial_value, ('seq', 'batch')) / token_total  81.2 us
    dot_general x4, matrix products, body(): jnp.dot(covariance, whole_basis, precision=lax.Precision.HIGHEST, preferr...  24.3 us
    another operation x30, local copies, waits for them, and re-layouts, orthonormal(): lax.linalg.triangular_solve(factor, images, left_side=False, lower=True,...  16.8 us
    all_gather x1, blocking collectives, body(): lax.all_gather(joint_rows, 'head', axis=1, tiled=True)  15.5 us
  transfers between devices with their start and end apart: 10, of which 9 were waited for; matrix products, arithmetic and copies ran while one was open for 0% of the time, Pallas kernels for 0%

profile of v1, /device:TPU:0, one launch (start us, length us, event | category | flops | bytes accessed | tf_op | source)
XLA Modules:
  0.0 685.6 jit_solution(11364646235048086768)
XLA Ops:
  7.4 7.8 %fusion.2 = f32[256,512]{1,0:T(8,128)} fusion(bf16[8192,256]{1,0:T(8,128)(2,1)} %param.12, bf16[8192,256]{1,0:T(8,128)(2,1)} %param.11, bf16[1,256,8192]{2,1,0:T(8,128)(2,1)} %param.9, f32[8192]{0:T(1024)} %param.10), kind=kOutput, calls=%fused_computation.12 | convolution fusion | flops 2170552320 | bytes 13139968 | tf_op jit(solution)/shard_map/dot_general | solution.py:68
  15.2 3.1 fusion.1
  18.4 5.9 psum.14
  24.5 8.2 %reduce-scatter.2.cloned.1.call-done = f32[128,512]{1,0:T(8,128)} async-done(((f32[256,512]{1,0:T(8,128)}), f32[128,512]{1,0:T(8,128)}) %reduce-scatter.2.cloned.1.call-update) | async-done | bytes 262160 | tf_op jit(solution)/shard_map/reduce_scatter | solution.py:67
  32.7 1.0 broadcast_multiply_fusion.4
  34.1 15.5 %all_gather.39 = bf16[128,2048]{0,1:T(8,128)(2,1)S(1)} all-gather(bf16[128,512]{0,1:T(8,128)(2,1)S(1)} %bitcast.164), channel_id=1, replica_groups=mesh['seq'=2,'batch'=4,'head'=4] {'head'}, dimensions={1}, use_global_device_ids=true | all-gather | bytes 655360 | tf_op jit(solution)/shard_map/all_gather | solution.py:82
  49.6 2.7 fusion.74
  52.9 81.2 %all-reduce.3.cloned.1.call-done = f32[512,2048]{1,0:T(8,128)} async-done(((f32[512,2048]{1,0:T(8,128)}), f32[512,2048]{1,0:T(8,128)}) %all-reduce.3.cloned.1.call-update) | async-done | bytes 4194320 | tf_op jit(solution)/shard_map/psum | solution.py:88
  134.1 6.1 fusion.15
  140.2 1.7 fusion.75
  142.3 27.7 %all-gather.21.cloned.1.call-done = f32[1024,256]{1,0:T(8,128)} async-done(((f32[256,256]{1,0:T(8,128)}), f32[1024,256]{1,0:T(8,128)}) %all-gather.21.cloned.1.call-update) | async-done | bytes 1048592 | tf_op jit(solution)/shard_map/all_gather | solution.py:98
  170.0 1.3 reduce_sum.46
  171.7 11.7 %cholesky.214 = f32[128,128]{1,0:T(8,128)S(1)} custom-call(f32[128,128]{1,0:T(8,128)S(1)} %cholesky.346), custom_call_target="Cholesky" | custom-call | tf_op jit(solution)/shard_map/jit(cholesky)/cholesky | solution.py:52
  183.5 9.8 %custom-call.17 = f32[1,128,128]{1,2,0:T(8,128)S(1)} custom-call(f32[1,128,128]{2,1,0:T(8,128)S(1)} %get-tuple-element.94), custom_call_target="InvertDiagBlocksLowerTriangular" | custom-call | tf_op jit(solution)/shard_map/jit(cholesky)/cholesky | solution.py:52
  193.8 11.7 %cholesky.231 = f32[128,128]{1,0:T(8,128)S(1)} custom-call(f32[128,128]{1,0:T(8,128)S(1)} %convolution_subtract_fusion.7), custom_call_target="Cholesky" | custom-call | tf_op jit(solution)/shard_map/jit(cholesky)/cholesky | solution.py:52
  205.5 0.7 compare_reduce_fusion.6
  207.6 4.5 while.8
  208.7 1.4 bitcast_dynamic-update-slice_fusion.8
  210.7 1.4 bitcast_dynamic-update-slice_fusion.8
  212.1 19.7 %custom-call.18 = f32[2,128,128]{1,2,0:T(8,128)S(1)} custom-call(f32[2,128,128]{2,1,0:T(8,128)S(1)} %get-tuple-element.33), custom_call_target="InvertDiagBlocksLowerTriangular" | custom-call | tf_op jit(solution)/shard_map/triangular_solve/custom-call.0 | solution.py:53
  233.2 0.8 pad_maximum_fusion
  234.1 44.9 %all-gather.15.cloned.1.call-done = f32[2048,256]{0,1:T(8,128)} async-done(((f32[512,256]{0,1:T(8,128)}), f32[2048,256]{0,1:T(8,128)}) %all-gather.15.cloned.1.call-update) | async-done | bytes 2097168 | tf_op jit(solution)/shard_map/all_gather | solution.py:33
  279.0 6.1 fusion.13
  285.1 1.7 fusion.76
  287.0 26.6 %all-gather.23.cloned.1.call-done = f32[1024,256]{1,0:T(8,128)} async-done(((f32[256,256]{1,0:T(8,128)}), f32[1024,256]{1,0:T(8,128)}) %all-gather.23.cloned.1.call-update) | async-done | bytes 1048592 | tf_op jit(solution)/shard_map/all_gather | solution.py:98
  313.6 1.3 reduce_sum.47
  315.3 11.7 %cholesky.248 = f32[128,128]{1,0:T(8,128)S(1)} custom-call(f32[128,128]{1,0:T(8,128)S(1)} %cholesky.349), custom_call_target="Cholesky" | custom-call | tf_op jit(solution)/shard_map/jit(cholesky)/cholesky | solution.py:52
  327.1 9.8 %custom-call.19 = f32[1,128,128]{1,2,0:T(8,128)S(1)} custom-call(f32[1,128,128]{2,1,0:T(8,128)S(1)} %get-tuple-element.90), custom_call_target="InvertDiagBlocksLowerTriangular" | custom-call | tf_op jit(solution)/shard_map/jit(cholesky)/cholesky | solution.py:52
  337.4 11.7 %cholesky.265 = f32[128,128]{1,0:T(8,128)S(1)} custom-call(f32[128,128]{1,0:T(8,128)S(1)} %convolution_subtract_fusion.6), custom_call_target="Cholesky" | custom-call | tf_op jit(solution)/shard_map/jit(cholesky)/cholesky | solution.py:52
  349.1 0.6 compare_reduce_fusion.4
  351.7 4.2 while.9
  352.6 1.4 bitcast_dynamic-update-slice_fusion.9
  354.5 1.4 bitcast_dynamic-update-slice_fusion.9
  355.9 19.7 %custom-call.20 = f32[2,128,128]{1,2,0:T(8,128)S(1)} custom-call(f32[2,128,128]{2,1,0:T(8,128)S(1)} %get-tuple-element.34), custom_call_target="InvertDiagBlocksLowerTriangular" | custom-call | tf_op jit(solution)/shard_map/triangular_solve/custom-call.0 | solution.py:53
  377.0 0.8 pad_maximum_fusion.1
  377.9 44.9 %all-gather.17.cloned.1.call-done = f32[2048,256]{0,1:T(8,128)} async-done(((f32[512,256]{0,1:T(8,128)}), f32[2048,256]{0,1:T(8,128)}) %all-gather.17.cloned.1.call-update) | async-done | bytes 2097168 | tf_op jit(solution)/shard_map/all_gather | solution.py:33
  422.8 6.1 fusion.11
  428.9 1.7 fusion.77
  431.0 26.5 %all-gather.25.cloned.1.call-done = f32[1024,256]{1,0:T(8,128)} async-done(((f32[256,256]{1,0:T(8,128)}), f32[1024,256]{1,0:T(8,128)}) %all-gather.25.cloned.1.call-update) | async-done | bytes 1048592 | tf_op jit(solution)/shard_map/all_gather | solution.py:98
  457.5 1.3 reduce_sum.48
  459.2 11.7 %cholesky.282 = f32[128,128]{1,0:T(8,128)S(1)} custom-call(f32[128,128]{1,0:T(8,128)S(1)} %cholesky.352), custom_call_target="Cholesky" | custom-call | tf_op jit(solution)/shard_map/jit(cholesky)/cholesky | solution.py:52
  470.9 9.8 %custom-call.21 = f32[1,128,128]{1,2,0:T(8,128)S(1)} custom-call(f32[1,128,128]{2,1,0:T(8,128)S(1)} %get-tuple-element.86), custom_call_target="InvertDiagBlocksLowerTriangular" | custom-call | tf_op jit(solution)/shard_map/jit(cholesky)/cholesky | solution.py:52
  481.2 11.7 %cholesky.299 = f32[128,128]{1,0:T(8,128)S(1)} custom-call(f32[128,128]{1,0:T(8,128)S(1)} %convolution_subtract_fusion.5), custom_call_target="Cholesky" | custom-call | tf_op jit(solution)/shard_map/jit(cholesky)/cholesky | solution.py:52
  493.0 0.6 compare_reduce_fusion.2
  493.6 0.6 compare_reduce_fusion.3
  495.6 16.0 %while.10 = (s32[]{:T(128)}, f32[256,256]{1,0:T(8,128)S(1)}, s32[2,2]{1,0:T(2,128)S(1)}, f32[2,128,128]{2,1,0:T(8,128)S(1)}, s32[]{:T(128)}) while((s32[]{:T(128)}, f32[256,256]{1,0:T(8,128)S(1)}, s32[2,2]{1,0:T(2,128)S(1)}, f32[2,128,128]{2,1,0:T(8,128)S(1)}, s32[]{:T(128)}) %tuple.112), condition=%wide.while_cond.clone.1, body=%wide.while_body.clone.1.sunk | while | flops 2 | bytes 131181 | solution.py:53
  508.3 1.4 bitcast_dynamic-update-slice_fusion.10
  510.2 1.4 bitcast_dynamic-update-slice_fusion.10
  511.6 19.7 %custom-call.22 = f32[2,128,128]{1,2,0:T(8,128)S(1)} custom-call(f32[2,128,128]{2,1,0:T(8,128)S(1)} %get-tuple-element.35), custom_call_target="InvertDiagBlocksLowerTriangular" | custom-call | tf_op jit(solution)/shard_map/triangular_solve/custom-call.0 | solution.py:53
  532.7 0.8 pad_maximum_fusion.2
  533.7 44.9 %all-gather.19.cloned.1.call-done = f32[2048,256]{0,1:T(8,128)} async-done(((f32[512,256]{0,1:T(8,128)}), f32[2048,256]{0,1:T(8,128)}) %all-gather.19.cloned.1.call-update) | async-done | bytes 2097168 | tf_op jit(solution)/shard_map/all_gather | solution.py:33
  578.6 6.1 fusion.9
  584.6 1.7 fusion.78
  586.4 26.8 %all-gather.27.cloned.1.call-done = f32[1024,256]{1,0:T(8,128)} async-done(((f32[256,256]{1,0:T(8,128)}), f32[1024,256]{1,0:T(8,128)}) %all-gather.27.cloned.1.call-update) | async-done | bytes 1048592 | tf_op jit(solution)/shard_map/all_gather | solution.py:98
  613.2 1.3 reduce_sum.49
  614.9 11.7 %cholesky.316 = f32[128,128]{1,0:T(8,128)S(1)} custom-call(f32[128,128]{1,0:T(8,128)S(1)} %cholesky.355), custom_call_target="Cholesky" | custom-call | tf_op jit(solution)/shard_map/jit(cholesky)/cholesky | solution.py:52
  626.6 9.8 %custom-call.23 = f32[1,128,128]{1,2,0:T(8,128)S(1)} custom-call(f32[1,128,128]{2,1,0:T(8,128)S(1)} %get-tuple-element.82), custom_call_target="InvertDiagBlocksLowerTriangular" | custom-call | tf_op jit(solution)/shard_map/jit(cholesky)/cholesky | solution.py:52
  636.9 11.7 %cholesky.333 = f32[128,128]{1,0:T(8,128)S(1)} custom-call(f32[128,128]{1,0:T(8,128)S(1)} %convolution_subtract_fusion.4), custom_call_target="Cholesky" | custom-call | tf_op jit(solution)/shard_map/jit(cholesky)/cholesky | solution.py:52
  648.7 0.7 compare_reduce_fusion
  651.4 4.1 while.11
  652.1 1.4 bitcast_dynamic-update-slice_fusion.11
  654.1 1.4 bitcast_dynamic-update-slice_fusion.11
  655.6 19.9 %custom-call.24 = f32[2,128,128]{1,2,0:T(8,128)S(1)} custom-call(f32[2,128,128]{2,1,0:T(8,128)S(1)} %get-tuple-element.36), custom_call_target="InvertDiagBlocksLowerTriangular" | custom-call | tf_op jit(solution)/shard_map/triangular_solve/custom-call.0 | solution.py:53
  676.9 1.0 copy.31
  (115 shorter events, 17.9 us)
Async XLA Ops:
  7.4 25.3 %reduce-scatter.2.cloned.1.call-start = ((), (), s32[]{:S(2)}) async-start(), calls=%async_computation.1 | async-start | bytes 786432 | tf_op jit(solution)/shard_map/reduce_scatter | solution.py:67
  15.2 9.1 %copy-start = (s32[1,128]{1,0:T(1,128)S(1)}, s32[1,128]{1,0:T(1,128)}, u32[]{:S(2)}) copy-start(s32[1,128]{1,0:T(1,128)} %param.13) | copy-start | bytes 1540
  15.2 118.9 %all-reduce.3.cloned.1.call-start = ((), (), s32[]{:S(2)}) async-start(), calls=%async_computation.2 | async-start | bytes 8388608 | tf_op jit(solution)/shard_map/psum | solution.py:88
  52.3 81.8 %all-gather.13.cloned.1.call-start = ((), (), s32[]{:S(2)}) async-start(), calls=%async_computation.3 | async-start | bytes 2621440 | tf_op jit(solution)/shard_map/all_gather | solution.py:33
  52.9 117.2 %all-gather.21.cloned.1.call-start = ((), (), s32[]{:S(2)}) async-start(), calls=%async_computation.7 | async-start | bytes 1310720 | tf_op jit(solution)/shard_map/all_gather | solution.py:98
  142.0 137.0 %all-gather.15.cloned.1.call-start = ((), (), s32[]{:S(2)}) async-start(), calls=%async_computation.4 | async-start | bytes 2621440 | tf_op jit(solution)/shard_map/all_gather | solution.py:33
  234.1 79.6 %all-gather.23.cloned.1.call-start = ((), (), s32[]{:S(2)}) async-start(), calls=%async_computation.8 | async-start | bytes 1310720 | tf_op jit(solution)/shard_map/all_gather | solution.py:98
  286.8 136.0 %all-gather.17.cloned.1.call-start = ((), (), s32[]{:S(2)}) async-start(), calls=%async_computation.5 | async-start | bytes 2621440 | tf_op jit(solution)/shard_map/all_gather | solution.py:33
  377.9 79.6 %all-gather.25.cloned.1.call-start = ((), (), s32[]{:S(2)}) async-start(), calls=%async_computation.9 | async-start | bytes 1310720 | tf_op jit(solution)/shard_map/all_gather | solution.py:98
  430.7 147.9 %all-gather.19.cloned.1.call-start = ((), (), s32[]{:S(2)}) async-start(), calls=%async_computation.6 | async-start | bytes 2621440 | tf_op jit(solution)/shard_map/all_gather | solution.py:33
  533.6 79.6 %all-gather.27.cloned.1.call-start = ((), (), s32[]{:S(2)}) async-start(), calls=%async_computation.10 | async-start | bytes 1310720 | tf_op jit(solution)/shard_map/all_gather | solution.py:98
Sparse Core Ops, SparseCore 0:
  15.3 17.3 reduce-scatter.1
  52.4 81.6 all-reduce.2
Sparse Core Ops, SparseCore 1:
  54.3 46.3 all-gather.12
  142.0 27.9 all-gather.20
  234.1 44.8 all-gather.14
  286.9 26.7 all-gather.22
  378.0 44.8 all-gather.16
  430.7 26.7 all-gather.24
  533.7 44.8 all-gather.18
  586.5 26.7 all-gather.26
